TPU v7x, 32 devices: a whole 2x2x4 slice. The times are simulated.
32 devices in a mesh: dp: 8 (over z, x), tensor: 4 (over y, core).
Axes of the slice: x: 2, y: 2, z: 4, core: 2. Of those that a mesh axis runs over, the one named last changes fastest.
Arguments:
- block_input: float32 [8192, 1536], P(('dp', 'tensor')), may hold values from -6 to 6
- cotangent: float32 [8192, 1536], P(('dp', 'tensor')), may hold values from -6 to 6
- norm_gain: float32 [1536], replicated, may hold values from 0.5 to 1.5
- gate_proj: bfloat16 [1536, 3072], P('dp', 'tensor'), may hold values from -0.15625 to 0.15625
- value_proj: bfloat16 [1536, 3072], P('dp', 'tensor'), may hold values from -0.15625 to 0.15625
- state_proj: bfloat16 [1536, 256], P('dp'), may hold values from -0.15625 to 0.15625
- step_proj: bfloat16 [1536, 48], P('dp', 'tensor'), may hold values from -0.15625 to 0.15625
- value_conv: float32 [4, 3072], P(None, 'tensor'), may hold values from -3 to 3
- value_conv_bias: float32 [3072], P('tensor'), may hold values from -3 to 3
- state_conv: float32 [4, 256], replicated, may hold values from -3 to 3
- state_conv_bias: float32 [256], replicated, may hold values from -3 to 3
- step_bias: float32 [48], P('tensor'), may hold values from -7 to -2.3
- decay_log: float32 [48], P('tensor'), may hold values from 0 to 2.77
- skip_gain: float32 [48], P('tensor'), may hold values from 0.5 to 2
- mixer_gain: float32 [3072], P('tensor'), may hold values from 0.5 to 1.5
- out_proj: bfloat16 [3072, 1536], P('tensor', 'dp'), may hold values from -0.109375 to 0.109375
Outputs:
- block_output: float32 [8192, 1536], P(('dp', 'tensor'))
- input_grad: float32 [8192, 1536], P(('dp', 'tensor'))
- norm_gain_grad: float32 [1536], replicated
- gate_proj_grad: float32 [1536, 3072], P('dp', 'tensor')
- value_proj_grad: float32 [1536, 3072], P('dp', 'tensor')
- state_proj_grad: float32 [1536, 256], P('dp')
- step_proj_grad: float32 [1536, 48], P('dp', 'tensor')
- value_conv_grad: float32 [4, 3072], P(None, 'tensor')
- value_conv_bias_grad: float32 [3072], P('tensor')
- state_conv_grad: float32 [4, 256], replicated
- state_conv_bias_grad: float32 [256], replicated
- step_bias_grad: float32 [48], P('tensor')
- decay_log_grad: float32 [48], P('tensor')
- skip_gain_grad: float32 [48], P('tensor')
- mixer_gain_grad: float32 [3072], P('tensor')
- out_proj_grad: float32 [3072, 1536], P('tensor', 'dp')
All inputs are finite; a program needn't handle non-finite values.
Results may differ from a plain program's by a relative error of at most 0.0088.
Values may be sent and summed in bfloat16 or wider, within the bound.
No kernel may reach another device: no remote copies, remote signals or barrier semaphores. Data moves between devices by JAX's collectives and lax.ppermute only.
A program may use at most 192 MiB of HBM per device.

v0:
```python
import jax
import jax.numpy as jnp
from jax import lax
from jax.sharding import PartitionSpec as P

INNER = 3072
HEADDIM = 64
NSTATE = 128
BLOCK_LEN = 256
SEQLEN = 1024
norm_eps = 1e-05
highest = lax.Precision.HIGHEST


def causal_conv(values, kernel, offset_bias, seq_len):
    rows_all, channels = values.shape
    seq_count = rows_all // seq_len
    taps_count = kernel.shape[0]
    shaped = values.reshape(seq_count, seq_len, channels)
    padded = jnp.pad(shaped, ((0, 0), (taps_count - 1, 0), (0, 0)))
    running = jnp.zeros_like(shaped) + offset_bias
    for offset in range(taps_count):
        running = running + padded[:, offset : offset + seq_len, :] * kernel[offset]
    return running.reshape(rows_all, channels)


def block_scan(inputs, b_rows, c_rows, steps_dt, rate, skip_term, seq_len, block_len):
    rows_all, heads_here, head_dim = inputs.shape
    state_dim = b_rows.shape[1]
    seq_count = rows_all // seq_len
    block_count = seq_len // block_len
    x_blocks = inputs.reshape(seq_count, block_count, block_len, heads_here, head_dim)
    b_blocks = b_rows.reshape(seq_count, block_count, block_len, state_dim)
    c_blocks = c_rows.reshape(seq_count, block_count, block_len, state_dim)
    dt_blocks = steps_dt.reshape(seq_count, block_count, block_len, heads_here)
    log_decay = jnp.cumsum(dt_blocks * rate, axis=2)
    block_end = log_decay[:, :, -1, :]
    position = jnp.arange(block_len)
    causal = (position[:, None] >= position[None, :])[None, None, :, :, None]
    gaps = log_decay[:, :, :, None, :] - log_decay[:, :, None, :, :]
    decay_mat = jnp.where(causal, jnp.exp(jnp.where(causal, gaps, 0.0)), 0.0)
    scores = jnp.einsum("scin,scjn->scij", c_blocks, b_blocks, precision=highest)
    mixing = scores[..., None] * decay_mat
    x_scaled = x_blocks * dt_blocks[..., None]
    y_inner = jnp.einsum("scijh,scjhp->scihp", mixing, x_scaled, precision=highest)
    to_end = jnp.exp(block_end[:, :, None, :] - log_decay)
    block_states = jnp.einsum(
        "scjn,scjhp->schnp", b_blocks, x_scaled * to_end[..., None], precision=highest
    )

    def advance(carried, pieces):
        piece_state, piece_end = pieces
        return (carried * jnp.exp(piece_end)[:, :, None, None] + piece_state, carried)

    start_state = jnp.zeros((seq_count, heads_here, state_dim, head_dim), jnp.float32)
    _, entering = lax.scan(
        advance, start_state, (jnp.moveaxis(block_states, 1, 0), jnp.moveaxis(block_end, 1, 0))
    )
    entering = jnp.moveaxis(entering, 0, 1)
    y_outer = (
        jnp.einsum("scin,schnp->scihp", c_blocks, entering, precision=highest)
        * jnp.exp(log_decay)[..., None]
    )
    result = y_inner + y_outer + x_blocks * skip_term[:, None]
    return result.reshape(rows_all, heads_here, head_dim)


def mixer(
    gate_pre,
    value_pre,
    state_pre,
    step_pre,
    value_conv,
    value_conv_bias,
    state_conv,
    state_conv_bias,
    step_bias,
    decay_log,
    skip_gain,
):
    x_conv = jax.nn.silu(causal_conv(value_pre, value_conv, value_conv_bias, SEQLEN))
    bc_conv = jax.nn.silu(causal_conv(state_pre, state_conv, state_conv_bias, SEQLEN))
    steps_dt = jax.nn.softplus(step_pre + step_bias)
    rows_all = x_conv.shape[0]
    scanned = block_scan(
        x_conv.reshape(rows_all, -1, HEADDIM),
        bc_conv[:, :NSTATE],
        bc_conv[:, NSTATE:],
        steps_dt,
        -jnp.exp(decay_log),
        skip_gain,
        SEQLEN,
        BLOCK_LEN,
    )
    return scanned.reshape(rows_all, -1) * jax.nn.silu(gate_pre)


def contract_rows(left, right):
    return lax.dot_general(
        left, right, (((0,), (0,)), ((), ())), preferred_element_type=jnp.float32
    )


def contract_cols(left, right):
    return lax.dot_general(
        left, right, (((1,), (1,)), ((), ())), preferred_element_type=jnp.float32
    )


def shards(
    block_input,
    cotangent,
    norm_gain,
    gate_proj,
    value_proj,
    state_proj,
    step_proj,
    value_conv,
    value_conv_bias,
    state_conv,
    state_conv_bias,
    step_bias,
    decay_log,
    skip_gain,
    mixer_gain,
    out_proj,
):
    rms_inv = lax.rsqrt(jnp.mean(block_input * block_input, axis=1, keepdims=True) + norm_eps)
    normed = (block_input * rms_inv * norm_gain).astype(jnp.bfloat16)
    gathered = lax.all_gather(normed, "tensor", axis=0, tiled=True)
    gate_full, value_full, state_full, step_full, out_full = (
        lax.all_gather(gate_proj, "dp", axis=0, tiled=True),
        lax.all_gather(value_proj, "dp", axis=0, tiled=True),
        lax.all_gather(state_proj, "dp", axis=0, tiled=True),
        lax.all_gather(step_proj, "dp", axis=0, tiled=True),
        lax.all_gather(out_proj, "dp", axis=1, tiled=True),
    )
    gate_pre = jnp.dot(gathered, gate_full, preferred_element_type=jnp.float32)
    value_pre = jnp.dot(gathered, value_full, preferred_element_type=jnp.float32)
    state_pre = jnp.dot(gathered, state_full, preferred_element_type=jnp.float32)
    step_pre = jnp.dot(gathered, step_full, preferred_element_type=jnp.float32)
    gated, pull_back = jax.vjp(
        mixer,
        gate_pre,
        value_pre,
        state_pre,
        step_pre,
        value_conv,
        value_conv_bias,
        state_conv,
        state_conv_bias,
        step_bias,
        decay_log,
        skip_gain,
    )
    row_squares = lax.psum(jnp.sum(gated * gated, axis=1, keepdims=True), "tensor")
    gate_inv = lax.rsqrt(row_squares / INNER + norm_eps)
    mixed_rows = (gated * gate_inv * mixer_gain).astype(jnp.bfloat16)
    block_output = block_input + lax.psum_scatter(
        jnp.dot(mixed_rows, out_full, preferred_element_type=jnp.float32),
        "tensor",
        scatter_dimension=0,
        tiled=True,
    )
    cot_low = cotangent.astype(jnp.bfloat16)
    cot_full = lax.all_gather(cot_low, "tensor", axis=0, tiled=True)
    mixed_grad = contract_cols(cot_full, out_full)
    gain_term = jnp.sum(mixed_grad * gated * gate_inv, axis=0)
    scaled_grad = mixed_grad * mixer_gain
    row_dot = lax.psum(jnp.sum(scaled_grad * gated, axis=1, keepdims=True), "tensor")
    gated_grad = gate_inv * scaled_grad - gated * gate_inv**3 * row_dot / INNER
    pulled = pull_back(gated_grad)
    state_total = lax.psum(pulled[2], "tensor")
    gate_low = pulled[0].astype(jnp.bfloat16)
    value_low = pulled[1].astype(jnp.bfloat16)
    state_low = state_total.astype(jnp.bfloat16)
    step_low = pulled[3].astype(jnp.bfloat16)
    first_flag = (lax.axis_index("tensor") == 0).astype(jnp.float32)
    running = (
        contract_cols(gate_low, gate_full)
        + contract_cols(value_low, value_full)
        + contract_cols(step_low, step_full)
    )
    normed_grad = lax.psum_scatter(
        running + first_flag * contract_cols(state_low, state_full),
        "tensor",
        scatter_dimension=0,
        tiled=True,
    )
    norm_term = jnp.sum(normed_grad * block_input * rms_inv, axis=0)
    scaled_in = normed_grad * norm_gain
    input_grad = (
        rms_inv * scaled_in
        - block_input * rms_inv**3 * jnp.mean(scaled_in * block_input, axis=1, keepdims=True)
        + cotangent
    )
    out_grad = contract_rows(mixed_rows, cot_full)
    proj_sums = (
        lax.psum_scatter(contract_rows(gathered, gate_low), "dp", scatter_dimension=0, tiled=True),
        lax.psum_scatter(contract_rows(gathered, value_low), "dp", scatter_dimension=0, tiled=True),
        lax.psum_scatter(contract_rows(gathered, state_low), "dp", scatter_dimension=0, tiled=True),
        lax.psum_scatter(contract_rows(gathered, step_low), "dp", scatter_dimension=0, tiled=True),
        lax.psum_scatter(out_grad, "dp", scatter_dimension=1, tiled=True),
    )
    gate_grad, value_grad, state_grad, step_grad, out_grad_owned = proj_sums
    small_sums = lax.psum((pulled[4], pulled[5], pulled[8], pulled[9], pulled[10], gain_term), "dp")
    shared_sums = lax.psum((norm_term, pulled[6], pulled[7]), ("dp", "tensor"))
    return (
        block_output,
        input_grad,
        shared_sums[0],
        gate_grad,
        value_grad,
        state_grad,
        step_grad,
        small_sums[0],
        small_sums[1],
        shared_sums[1],
        shared_sums[2],
        small_sums[2],
        small_sums[3],
        small_sums[4],
        small_sums[5],
        out_grad_owned,
    )


def solution(mesh):
    in_specs = (
        P(("dp", "tensor"), None),
        P(("dp", "tensor"), None),
        P(),
        P("dp", "tensor"),
        P("dp", "tensor"),
        P("dp", None),
        P("dp", "tensor"),
        P(None, "tensor"),
        P("tensor"),
        P(),
        P(),
        P("tensor"),
        P("tensor"),
        P("tensor"),
        P("tensor"),
        P("tensor", "dp"),
    )
    out_specs = (
        P(("dp", "tensor"), None),
        P(("dp", "tensor"), None),
        P(),
        P("dp", "tensor"),
        P("dp", "tensor"),
        P("dp", None),
        P("dp", "tensor"),
        P(None, "tensor"),
        P("tensor"),
        P(),
        P(),
        P("tensor"),
        P("tensor"),
        P("tensor"),
        P("tensor"),
        P("tensor", "dp"),
    )
    return jax.shard_map(shards, mesh=mesh, in_specs=in_specs, out_specs=out_specs, check_vma=False)
```

profile of v0, /device:TPU:0, one launch (start us, length us, event | category | flops | bytes accessed | tf_op | source)
XLA Modules:
  0.0 941.6 jit_solution(11002507970807550462)
XLA Ops:
  16.6 32.4 %all-gather = bf16[8,192,12]{1,2,0:T(8,128)(2,1)S(1)} all-gather(bf16[1,192,12]{1,2,0:T(8,128)(2,1)S(1)} %bitcast.399), channel_id=1, replica_groups=mesh['dp'=8,'tensor'=4] {'dp'}, dimensions={0}, use_global_device_ids=true | all-gather | bytes 41472 | tf_op jit(solution)/shard_map/all_gather | solution.py:135
  49.1 33.3 %all_gather.24 = bf16[1536,256]{1,0:T(8,128)(2,1)S(1)} all-gather(bf16[192,256]{1,0:T(8,128)(2,1)S(1)} %copy-done.34), channel_id=1, replica_groups=mesh['dp'=8,'tensor'=4] {'dp'}, dimensions={0}, use_global_device_ids=true | all-gather | bytes 884736 | tf_op jit(solution)/shard_map/all_gather | solution.py:134
  130.4 13.9 %while.36 = (s32[]{:T(128)}, f32[1,12,128,64]{3,2,1,0:T(8,128)S(1)}, f32[4,1,12,128,64]{4,3,2,1,0:T(8,128)}, f32[4,1,12]{2,1,0:T(1,128)}, f32[4,1,12,1,1]{2,4,3,...) while((s32[]{:T(128)}, ...), condition=%wide.region_4.5_spmd.clone, body=%wide.region_3.4_spmd.clone.sunk | while | flops 393219 | bytes 3933504 | solution.py:56
  159.1 16.4 %fusion.33 = f32[1,4,256,12,64]{2,4,3,1,0:T(8,128)S(1)} fusion(f32[4,256,12,64]{1,3,2,0:T(8,128)S(1)} %bitcast.363, f32[4,256,12]{1,2,0:T(8,128)S(1)} %copy.382, f32[4,256,256]{2,1,0:T(8,128)S(1)} %fusion.127, pred[256,256]{1,0:T(8,128)(4,1)S(1)} %copy-done.43, f32[12]{0:T(128)S(1)} %copy-done.67, f32[4,256,12]{1,2,0:T(8,128)S(1)} %copy.391, ...), kind=kOutput, calls=%fused_computation.59 | convolution fusion | flops 2438725632 | bytes 13844528 | tf_op jit(solution)/shard_map/jvp(scijh,scjhp->scihp)/dot_general | solution.py:45
  183.5 9.2 multiply_reduce_fusion.7
  198.8 9.4 all-gather.13.cloned.1.call-done
  208.2 29.1 %all-gather.15.cloned.1.call-done = bf16[1024,1536]{1,0:T(8,128)(2,1)} async-done(((bf16[256,1536]{1,0:T(8,128)(2,1)}), bf16[1024,1536]{1,0:T(8,128)(2,1)}) %all-gather.15.cloned.1.call-update) | async-done | bytes 3145744 | tf_op jit(solution)/shard_map/all_gather | solution.py:166
  237.3 8.0 multiply_reduce_fusion
  251.1 7.3 fusion.25
  277.2 10.9 %fusion.66 = f32[4,256,128]{2,1,0:T(8,128)} fusion(f32[4,256,12,64]{1,0,3,2:T(4,128)S(1)} %copy-done.1, f32[4,256,12]{1,2,0:T(8,128)S(1)} %copy.391, f32[4,1,12,128,64]{4,3,2,1,0:T(8,128)S(1)} %copy-done), kind=kOutput, calls=%fused_computation.120 | convolution fusion | flops 1208745984 | bytes 5292032 | tf_op jit(solution)/shard_map/transpose(jvp(scin,schnp->scihp))/dot_general | solution.py:61
  294.8 20.0 %while.37 = (s32[]{:T(128)}, f32[1,12,128,64]{3,2,1,0:T(8,128)S(1)}, f32[4,1,12,128,64]{4,3,2,1,0:T(8,128)}, f32[4,1,12]{2,1,0:T(1,128)S(1)}, f32[4,1,12,128,64]...) while((s32[]{:T(128)}, ...), condition=%wide.region_12.13_spmd.clone, body=%wide.region_10.12_spmd.clone.sunk | while | flops 589828 | bytes 4326800 | solution.py:56
  314.7 21.2 %fusion.12 = (f32[4,256,12]{1,2,0:T(8,128)S(1)}, f32[4,256,12]{1,2,0:T(8,128)S(1)}, f32[4,256,256]{2,1,0:T(8,128)S(1)}) fusion(f32[4,256,12]{1,2,0:T(8,128)S(1)} %copy.382, f32[4,256,256]{2,1,0:T(8,128)} %copy-done.30, pred[256,256]{1,0:T(8,128)(4,1)S(1)} %copy-done.43, f32[4,256,12,64]{1,0,3,2:T(4,128)} %reshape.652, f32[4,256,12]{1,2,0:T(8,128)S(1)} %copy-done.37, ...), kind=kOutput, calls=%fused_computation.29 | convolution fusion | flops 2454167552 | bytes 8650752 | tf_op jit(solution)/shard_map/transpose(jvp(scijh,scjhp->scihp))/dot_general | solution.py:45
  346.2 13.9 %fusion.43 = (f32[4,256,12]{1,2,0:T(8,128)S(1)}, f32[4,256,12]{1,2,0:T(8,128)S(1)}, f32[1,4,256,12,64]{2,4,3,1,0:T(8,128)}) fusion(f32[4,12,64,256]{3,2,1,0:T(8,128)S(1)} %fusion.41, f32[4,256,12]{1,2,0:T(8,128)S(1)} %copy-done.38, f32[1,4,256,12,64]{2,1,4,3,0:T(4,128)S(1)} %copy-done.22, f32[12]{0:T(128)S(1)} %copy-done.67, ...), kind=kOutput, calls=%fused_computation.74 | convolution fusion | flops 2439487488 | bytes 17088560 | tf_op jit(solution)/shard_map/transpose(jvp(scijh,scjhp->scihp))/dot_general | solution.py:45
  363.6 9.9 %reduce-window.16 = f32[1,4,12,2,128]{4,2,3,1,0:T(8,128)S(1)} reduce-window(f32[1,4,12,2,128]{4,2,3,1,0:T(8,128)S(1)} %copy.421, f32[]{:T(128)} %constant.104.clone.1), window={size=1x1x1x1x128 pad=0_0x0_0x0_0x0_0x0_127}, to_apply=%region_19.20 | reduce-window | flops 1560576 | bytes 98308 | tf_op jit(solution)/shard_map/reduce-window.2
  401.7 26.7 %all-reduce.24 = bf16[1024,256]{1,0:T(8,128)(2,1)} all-reduce(f32[1024,256]{1,0:T(8,128)} %fusion.79), channel_id=1, replica_groups=mesh['dp'=8,'tensor'=4] {'tensor'}, use_global_device_ids=true, to_apply=%region_22.23 | all-reduce | flops 262144 | bytes 1572864 | tf_op jit(solution)/shard_map/psum | solution.py:173
  443.6 7.9 fusion.115
  456.2 8.3 fusion.114
  472.1 7.2 fusion.132
  492.3 37.9 %all-reduce.22 = (f32[4,768]{1,0:T(4,128)}, f32[768]{0:T(1024)}, f32[12]{0:T(128)}, f32[12]{0:T(128)}, f32[12]{0:T(128)}, /*index=5*/f32[768]{0:T(1024)}) all-reduce(f32[4,768]{1,0:T(4,128)S(1)} %pad_add_fusion.6, f32[768]{0:T(1024)S(1)} %get-tuple-element.387, ...), channel_id=1, replica_groups=mesh['dp'=8,'tensor'=4] {'dp'}, use_global_device_ids=true, to_apply=%region_35.36 | all-reduce | flops 4644 | bytes 37152 | tf_op jit(solution)/shard_map/psum | solution.py:206
  536.6 37.8 %all-reduce.21 = (f32[1536]{0:T(1024)}, f32[4,256]{1,0:T(4,128)}, f32[256]{0:T(256)}) all-reduce(f32[1536]{0:T(1024)S(1)} %get-tuple-element.388, f32[4,256]{1,0:T(4,128)S(1)} %pad_add_fusion.7, f32[256]{0:T(256)S(1)} %get-tuple-element.395), channel_id=1, replica_groups=mesh['dp'=8,'tensor'=4] {'dp','tensor'}, use_global_device_ids=true, to_apply=%region_26.27 | all-reduce | flops 2816 | bytes 22528 | tf_op jit(solution)/shard_map/psum | solution.py:207
  578.3 58.5 %reduce-scatter.18.cloned.1.call-done = f32[192,256]{1,0:T(8,128)} async-done(((f32[1536,256]{1,0:T(8,128)}), f32[192,256]{1,0:T(8,128)}) %reduce-scatter.18.cloned.1.call-update) | async-done | bytes 196624 | tf_op jit(solution)/shard_map/reduce_scatter | solution.py:201
  636.8 98.6 %reduce-scatter.20.cloned.1.call-done = f32[768,192]{0,1:T(8,128)} async-done(((f32[768,1536]{0,1:T(8,128)}), f32[768,192]{0,1:T(8,128)}) %reduce-scatter.20.cloned.1.call-update) | async-done | bytes 589840 | tf_op jit(solution)/shard_map/reduce_scatter | solution.py:203
  735.4 99.6 %reduce-scatter.14.cloned.1.call-done = f32[192,768]{1,0:T(8,128)} async-done(((f32[1536,768]{1,0:T(8,128)}), f32[192,768]{1,0:T(8,128)}) %reduce-scatter.14.cloned.1.call-update) | async-done | bytes 589840 | tf_op jit(solution)/shard_map/reduce_scatter | solution.py:199
  835.0 99.4 %reduce-scatter.16.cloned.1.call-done = f32[192,768]{1,0:T(8,128)} async-done(((f32[1536,768]{1,0:T(8,128)}), f32[192,768]{1,0:T(8,128)}) %reduce-scatter.16.cloned.1.call-update) | async-done | bytes 589840 | tf_op jit(solution)/shard_map/reduce_scatter | solution.py:200
  (345 shorter events, 242.7 us)
Async XLA Ops:
  7.2 75.2 %all-gather.7.cloned.1.call-start = ((), (), s32[]{:S(2)}) async-start(), calls=%async_computation.7 | async-start | bytes 3932160 | tf_op jit(solution)/shard_map/all_gather | solution.py:130
  12.6 69.8 %copy-start.63 = (f32[12]{0:T(128)S(1)}, f32[12]{0:T(128)}, u32[]{:S(2)}) copy-start(f32[12]{0:T(128)} %param.31) | copy-start | bytes 148
  12.6 89.5 %all-gather.9.cloned.1.call-start = ((), (), s32[]{:S(2)}) async-start(), calls=%async_computation.8 | async-start | bytes 2654208 | tf_op jit(solution)/shard_map/all_gather | solution.py:133
  13.4 170.1 %all-gather.11.cloned.1.call-start = ((), (), s32[]{:S(2)}) async-start(), calls=%async_computation.9 | async-start | bytes 2654208 | tf_op jit(solution)/shard_map/all_gather | solution.py:132
  14.1 194.1 %all-gather.13.cloned.1.call-start = ((), (), s32[]{:S(2)}) async-start(), calls=%async_computation.10 | async-start | bytes 2654208 | tf_op jit(solution)/shard_map/all_gather | solution.py:136
  14.7 222.6 %all-gather.15.cloned.1.call-start = ((), (), s32[]{:S(2)}) async-start(), calls=%async_computation.12 | async-start | bytes 3932160 | tf_op jit(solution)/shard_map/all_gather | solution.py:166
  15.7 517.4 %reduce-scatter.22.cloned.1.call-start = ((), (), s32[]{:S(2)}) async-start(), calls=%async_computation.18 | async-start | bytes 884736
  16.5 69.8 %copy-start.61 = (f32[12]{0:T(128)}, f32[12]{0:T(128)S(1)}, u32[]{:S(2)}) copy-start(f32[12]{0:T(128)S(1)} %exponential_negate_fusion) | copy-start | bytes 148
  16.5 76.8 %copy-start.48 = (f32[1,256]{1,0:T(1,128)}, f32[1,256]{1,0:T(1,128)S(1)}, u32[]{:S(2)}) copy-start(f32[1,256]{1,0:T(1,128)S(1)} %get-tuple-element.473) | copy-start | bytes 3076
  16.5 76.8 %copy-start.50 = (f32[1,256]{1,0:T(1,128)}, f32[1,256]{1,0:T(1,128)S(1)}, u32[]{:S(2)}) copy-start(f32[1,256]{1,0:T(1,128)S(1)} %get-tuple-element.474) | copy-start | bytes 3076
  16.5 76.8 %copy-start.52 = (f32[1,256]{1,0:T(1,128)}, f32[1,256]{1,0:T(1,128)S(1)}, u32[]{:S(2)}) copy-start(f32[1,256]{1,0:T(1,128)S(1)} %get-tuple-element.475) | copy-start | bytes 3076
  16.6 76.8 %copy-start.54 = (f32[1,256]{1,0:T(1,128)}, f32[1,256]{1,0:T(1,128)S(1)}, u32[]{:S(2)}) copy-start(f32[1,256]{1,0:T(1,128)S(1)} %get-tuple-element.476) | copy-start | bytes 3076
  149.6 165.1 %copy-start.41 = (f32[4,256,12]{1,2,0:T(8,128)}, f32[4,256,12]{1,2,0:T(8,128)S(1)}, u32[]{:S(2)}) copy-start(f32[4,256,12]{1,2,0:T(8,128)S(1)} %copy.382) | copy-start | bytes 147460
  183.5 53.8 %copy-start.58 = (f32[768]{0:T(1024)S(1)}, f32[768]{0:T(1024)}, u32[]{:S(2)}) copy-start(f32[768]{0:T(1024)} %param.34) | copy-start | bytes 9220
  380.0 154.7 %reduce-scatter.12.cloned.1.call-start = ((), (), s32[]{:S(2)}) async-start(), calls=%async_computation.13 | async-start | bytes 7864320 | tf_op jit(solution)/shard_map/reduce_scatter | solution.py:184
  443.4 131.0 %reduce-scatter.10.cloned.1.call-start = ((), (), s32[]{:S(2)}) async-start(), calls=%async_computation.11 | async-start | bytes 7864320 | tf_op jit(solution)/shard_map/reduce_scatter | solution.py:159
  451.5 185.3 %reduce-scatter.18.cloned.1.call-start = ((), (), s32[]{:S(2)}) async-start(), calls=%async_computation.16 | async-start | bytes 1769472 | tf_op jit(solution)/shard_map/reduce_scatter | solution.py:201
  456.2 279.3 %reduce-scatter.20.cloned.1.call-start = ((), (), s32[]{:S(2)}) async-start(), calls=%async_computation.17 | async-start | bytes 5308416 | tf_op jit(solution)/shard_map/reduce_scatter | solution.py:203
  464.6 370.4 %reduce-scatter.14.cloned.1.call-start = ((), (), s32[]{:S(2)}) async-start(), calls=%async_computation.14 | async-start | bytes 5308416 | tf_op jit(solution)/shard_map/reduce_scatter | solution.py:199
  471.9 462.6 %reduce-scatter.16.cloned.1.call-start = ((), (), s32[]{:S(2)}) async-start(), calls=%async_computation.15 | async-start | bytes 5308416 | tf_op jit(solution)/shard_map/reduce_scatter | solution.py:200
  487.3 47.5 %copy-start.35 = (f32[1536]{0:T(1024)S(1)}, f32[1536]{0:T(1024)}, u32[]{:S(2)}) copy-start(f32[1536]{0:T(1024)} %param.22) | copy-start | bytes 18436
  487.3 47.5 %copy-start.46 = (f32[256]{0:T(256)S(1)}, f32[256]{0:T(256)}, u32[]{:S(2)}) copy-start(f32[256]{0:T(256)} %copy-done.45) | copy-start | bytes 3076
  492.1 82.3 %copy-start.15 = (f32[256,1536]{1,0:T(8,128)S(1)}, f32[256,1536]{1,0:T(8,128)}, u32[]{:S(2)}) copy-start(f32[256,1536]{1,0:T(8,128)} %param.21) | copy-start | bytes 4718596
  492.1 82.3 %copy-start.59 = (f32[256]{0:T(256)S(1)}, f32[256]{0:T(256)}, u32[]{:S(2)}) copy-start(f32[256]{0:T(256)} %get-tuple-element.477) | copy-start | bytes 3076
  (60 other events, 457.7 us)
Sparse Core Ops, SparseCore 0:
  12.8 31.2 all-gather.6
  46.2 55.8 all-gather.8
  104.3 51.6 all-gather.10
  158.0 50.1 all-gather.12
  210.2 27.0 all-gather.14
  380.1 64.2 reduce-scatter.21
  447.0 57.9 reduce-scatter.11
  507.5 59.6 reduce-scatter.9
  571.2 65.6 reduce-scatter.17
  640.9 94.5 reduce-scatter.19
  739.7 95.3 reduce-scatter.13
  839.1 95.3 reduce-scatter.15
where the time goes:
time: 953 us; the launch traced here: 942 us
  waiting for transfers between devices  403 us (42%)
  blocking collectives  180 us (19%)
  matrix products  169 us (18%)
  local copies, waits for them, and re-layouts  95.7 us (10%)
  other arithmetic  77.9 us (8%)
  between operations  15.6 us (2%)
    reduce_scatter x1, waiting for transfers between devices, shards(): lax.psum_scatter(contract_rows(gathered, gate_low), 'dp', scatter_dimensi...  99.6 us
    reduce_scatter x1, waiting for transfers between devices, shards(): lax.psum_scatter(contract_rows(gathered, value_low), 'dp', scatter_dimens...  99.4 us
    reduce_scatter x1, waiting for transfers between devices, shards(): lax.psum_scatter(out_grad, 'dp', scatter_dimension=1, tiled=True)  98.6 us
    reduce_scatter x1, waiting for transfers between devices, shards(): lax.psum_scatter(contract_rows(gathered, state_low), 'dp', scatter_dimens...  58.5 us
    dot_general x3, matrix products, block_scan(): jnp.einsum('scijh,scjhp->scihp', mixing, x_scaled, precision=highest)  51.6 us
    psum x1, blocking collectives, shards(): lax.psum((pulled[4], pulled[5], pulled[8], pulled[9], pulled[10], gain_te...  37.9 us
    psum x1, blocking collectives, shards(): shared_sums = lax.psum((norm_term, pulled[6], pulled[7]), ('dp', 'tensor'))  37.8 us
    all_gather x1, blocking collectives, shards(): lax.all_gather(state_proj, 'dp', axis=0, tiled=True)  33.3 us
  transfers between devices with their start and end apart: 12, of which 7 were waited for; matrix products, arithmetic and copies ran while one was open for 20% of the time, Pallas kernels for 0%

commit v1 on v0

--- a/solution.py
+++ b/solution.py
@@ -170,7 +170,9 @@
     row_dot = lax.psum(jnp.sum(scaled_grad * gated, axis=1, keepdims=True), "tensor")
     gated_grad = gate_inv * scaled_grad - gated * gate_inv**3 * row_dot / INNER
     pulled = pull_back(gated_grad)
-    state_total = lax.psum(pulled[2], "tensor")
+    x = pulled[2]
+    parts = lax.all_gather(x, "tensor", axis=0, tiled=False)
+    state_total = parts.sum(axis=0)
     gate_low = pulled[0].astype(jnp.bfloat16)
     value_low = pulled[1].astype(jnp.bfloat16)
     state_low = state_total.astype(jnp.bfloat16)

time: 953 us -> 991 us (1.040)
  waiting for transfers between devices: 403 us -> 437 us
  blocking collectives: 180 us -> 156 us
  matrix products: 169 us -> 187 us
  other arithmetic: 77.9 us -> 89.5 us
    psum x1 -> x0, blocking collectives: 26.7 us -> none  [shards(): state_total = lax.psum(pulled[2], 'tensor')]
    reduce_scatter x1, waiting for transfers between devices: 0.01 us -> 20.2 us  [shards(): lax.psum_scatter(jnp.dot(mixed_rows, out_full, preferred_element_type=jnp...]
    dot_general x5, matrix products: 20.8 us -> 32.1 us  [contract_cols(): lax.dot_general(left, right, (((1,), (1,)), ((), ())), preferred_element_...]
    reduce_scatter x1, waiting for transfers between devices: 58.5 us -> 69 us  [shards(): lax.psum_scatter(contract_rows(gathered, state_low), 'dp', scatter_dimens...]
  transfers between devices with their start and end apart: 12 -> 13, of which waited for: 7 -> 9; matrix products, arithmetic and copies ran while one was open for 20% -> 26% of each run, Pallas kernels for 0% -> 0%
where the time goes in v1:
time: 991 us; the launch traced here: 980 us
  waiting for transfers between devices  437 us (44%)
  matrix products  187 us (19%)
  blocking collectives  156 us (16%)
  local copies, waits for them, and re-layouts  94.6 us (10%)
  other arithmetic  89.5 us (9%)
  between operations  15.6 us (2%)
    reduce_scatter x1, waiting for transfers between devices, shards(): lax.psum_scatter(contract_rows(gathered, gate_low), 'dp', scatter_dimensi...  99.6 us
    reduce_scatter x1, waiting for transfers between devices, shards(): lax.psum_scatter(contract_rows(gathered, value_low), 'dp', scatter_dimens...  98.7 us
    reduce_scatter x1, waiting for transfers between devices, shards(): lax.psum_scatter(out_grad, 'dp', scatter_dimension=1, tiled=True)  95.3 us
    reduce_scatter x1, waiting for transfers between devices, shards(): lax.psum_scatter(contract_rows(gathered, state_low), 'dp', scatter_dimens...  69 us
    dot_general x3, matrix products, block_scan(): jnp.einsum('scijh,scjhp->scihp', mixing, x_scaled, precision=highest)  52.7 us
    psum x1, blocking collectives, shards(): shared_sums = lax.psum((norm_term, pulled[6], pulled[7]), ('dp', 'tensor'))  40.1 us
    psum x1, blocking collectives, shards(): lax.psum((pulled[4], pulled[5], pulled[8], pulled[9], pulled[10], gain_te...  37.9 us
    all_gather x1, blocking collectives, shards(): lax.all_gather(state_proj, 'dp', axis=0, tiled=True)  33.4 us
  transfers between devices with their start and end apart: 13, of which 9 were waited for; matrix products, arithmetic and copies ran while one was open for 26% of the time, Pallas kernels for 0%

profile of v1, /device:TPU:0, one launch (start us, length us, event | category | flops | bytes accessed | tf_op | source)
XLA Modules:
  0.0 979.7 jit_solution(4446598101532636848)
XLA Ops:
  16.1 32.4 %all-gather = bf16[8,192,12]{1,2,0:T(8,128)(2,1)S(1)} all-gather(bf16[1,192,12]{1,2,0:T(8,128)(2,1)S(1)} %bitcast.395), channel_id=1, replica_groups=mesh['dp'=8,'tensor'=4] {'dp'}, dimensions={0}, use_global_device_ids=true | all-gather | bytes 41472 | tf_op jit(solution)/shard_map/all_gather | solution.py:135
  48.6 33.4 %all_gather.27 = bf16[1536,256]{1,0:T(8,128)(2,1)S(1)} all-gather(bf16[192,256]{1,0:T(8,128)(2,1)S(1)} %copy-done.33), channel_id=1, replica_groups=mesh['dp'=8,'tensor'=4] {'dp'}, dimensions={0}, use_global_device_ids=true | all-gather | bytes 884736 | tf_op jit(solution)/shard_map/all_gather | solution.py:134
  129.2 11.9 %while.36 = (s32[]{:T(128)}, f32[1,12,128,64]{3,2,1,0:T(8,128)S(1)}, f32[4,1,12,128,64]{4,3,2,1,0:T(8,128)}, f32[4,1,12]{2,1,0:T(1,128)S(1)}, f32[4,1,12,1,1]{2,...) while((s32[]{:T(128)}, ...), condition=%wide.region_4.5_spmd.clone, body=%wide.region_3.4_spmd.clone.sunk | while | flops 393219 | bytes 3934432 | solution.py:56
  155.8 16.7 %fusion.33 = f32[1,4,256,12,64]{2,4,3,1,0:T(8,128)S(1)} fusion(f32[4,256,12,64]{1,3,2,0:T(8,128)S(1)} %bitcast.359, f32[4,256,12]{1,2,0:T(8,128)S(1)} %copy.382, f32[4,256,256]{2,1,0:T(8,128)S(1)} %fusion.126, pred[256,256]{1,0:T(8,128)(4,1)S(1)} %copy-done.43, f32[12]{0:T(128)S(1)} %copy-done.86, f32[4,256,12]{1,2,0:T(8,128)S(1)} %copy.391, ...), kind=kOutput, calls=%fused_computation.59 | convolution fusion | flops 2438725632 | bytes 13844528 | tf_op jit(solution)/shard_map/jvp(scijh,scjhp->scihp)/dot_general | solution.py:45
  180.4 9.3 multiply_reduce_fusion.7
  195.8 12.0 %all-gather.14.cloned.1.call-done = bf16[768,1536]{0,1:T(8,128)(2,1)} async-done(((bf16[768,192]{0,1:T(8,128)(2,1)}), bf16[768,1536]{0,1:T(8,128)(2,1)}) %all-gather.14.cloned.1.call-update) | async-done | bytes 2359312 | tf_op jit(solution)/shard_map/all_gather | solution.py:136
  207.8 29.1 %all-gather.16.cloned.1.call-done = bf16[1024,1536]{1,0:T(8,128)(2,1)} async-done(((bf16[256,1536]{1,0:T(8,128)(2,1)}), bf16[1024,1536]{1,0:T(8,128)(2,1)}) %all-gather.16.cloned.1.call-update) | async-done | bytes 3145744 | tf_op jit(solution)/shard_map/all_gather | solution.py:166
  236.9 8.5 multiply_reduce_fusion
  272.5 13.9 %fusion.66 = f32[4,256,128]{2,1,0:T(8,128)} fusion(f32[4,256,12,64]{1,0,3,2:T(4,128)} %reshape.664, f32[4,256,12]{1,2,0:T(8,128)S(1)} %copy.391, f32[4,1,12,128,64]{4,3,2,1,0:T(8,128)} %get-tuple-element.618), kind=kOutput, calls=%fused_computation.120 | convolution fusion | flops 1208745984 | bytes 5292032 | tf_op jit(solution)/shard_map/transpose(jvp(scin,schnp->scihp))/dot_general | solution.py:61
  292.9 19.9 %while.37 = (s32[]{:T(128)}, f32[1,12,128,64]{3,2,1,0:T(8,128)S(1)}, f32[4,1,12,128,64]{4,3,2,1,0:T(8,128)}, f32[4,1,12]{2,1,0:T(1,128)S(1)}, f32[4,1,12,128,64]...) while((s32[]{:T(128)}, ...), condition=%wide.region_12.13_spmd.clone, body=%wide.region_10.12_spmd.clone.sunk | while | flops 589828 | bytes 4326800 | solution.py:56
  313.3 22.1 %fusion.12 = (f32[4,256,12]{1,2,0:T(8,128)S(1)}, f32[4,256,12]{1,2,0:T(8,128)}, f32[4,256,256]{2,1,0:T(8,128)S(1)}) fusion(f32[4,256,12]{1,2,0:T(8,128)S(1)} %copy.382, f32[4,256,256]{2,1,0:T(8,128)} %copy-done.25, pred[256,256]{1,0:T(8,128)(4,1)S(1)} %copy-done.43, f32[4,256,12,64]{1,0,3,2:T(4,128)} %reshape.649, f32[4,256,12]{1,2,0:T(8,128)S(1)} %copy-done.36, ...), kind=kOutput, calls=%fused_computation.29 | convolution fusion | flops 2454167552 | bytes 8650752 | tf_op jit(solution)/shard_map/transpose(jvp(scijh,scjhp->scihp))/dot_general | solution.py:45
  356.8 13.9 %fusion.43 = (f32[4,256,12]{1,2,0:T(8,128)S(1)}, f32[4,256,12]{1,2,0:T(8,128)S(1)}, f32[1,4,256,12,64]{2,4,3,1,0:T(8,128)}) fusion(f32[4,12,64,256]{3,2,1,0:T(8,128)S(1)} %fusion.41, f32[4,256,12]{1,2,0:T(8,128)S(1)} %copy-done.37, f32[1,4,256,12,64]{2,1,4,3,0:T(4,128)S(1)} %copy-done.20, f32[12]{0:T(128)S(1)} %copy-done.87, ...), kind=kOutput, calls=%fused_computation.74 | convolution fusion | flops 2439487488 | bytes 17088560 | tf_op jit(solution)/shard_map/transpose(jvp(scijh,scjhp->scihp))/dot_general | solution.py:45
  375.1 9.9 %reduce-window.16 = f32[1,4,12,2,128]{4,2,3,1,0:T(8,128)S(1)} reduce-window(f32[1,4,12,2,128]{4,2,3,1,0:T(8,128)S(1)} %copy.421, f32[]{:T(128)} %constant.104.clone.1), window={size=1x1x1x1x128 pad=0_0x0_0x0_0x0_0x0_127}, to_apply=%region_19.20 | reduce-window | flops 1560576 | bytes 98308 | tf_op jit(solution)/shard_map/reduce-window.2
  436.1 10.4 %multiply_add_fusion = f32[1024,1536]{1,0:T(8,128)} fusion(f32[1024,1536]{1,0:T(8,128)} %fusion.101, f32[1024,1536]{1,0:T(8,128)} %fusion.128, f32[1024,1536]{1,0:T(8,128)} %fusion.129, bf16[1536,256]{1,0:T(8,128)(2,1)S(1)} %copy-done.17, f32[]{:T(128)S(6)} %convert_element_type.35, bf16[1024,256]{1,0:T(8,128)(2,1)S(1)} %reduce_sum.282), kind=kOutput, calls=%fused_computation.30 | convolution fusion | flops 811597824 | bytes 26476548 | tf_op jit(solution)/shard_map/dot_general | solution.py:105
  447.2 7.9 fusion.114
  455.2 7.8 fusion.113
  489.9 7.5 fusion.38
  497.6 37.9 %all-reduce.22 = (f32[4,768]{1,0:T(4,128)}, f32[768]{0:T(1024)}, f32[12]{0:T(128)}, f32[12]{0:T(128)}, f32[12]{0:T(128)}, /*index=5*/f32[768]{0:T(1024)}) all-reduce(f32[4,768]{1,0:T(4,128)S(1)} %pad_add_fusion.6, f32[768]{0:T(1024)S(1)} %get-tuple-element.387, ...), channel_id=1, replica_groups=mesh['dp'=8,'tensor'=4] {'dp'}, use_global_device_ids=true, to_apply=%region_35.36 | all-reduce | flops 4644 | bytes 37152 | tf_op jit(solution)/shard_map/psum | solution.py:208
  545.3 40.1 %all-reduce.21 = (f32[1536]{0:T(1024)}, f32[4,256]{1,0:T(4,128)}, f32[256]{0:T(256)}) all-reduce(f32[1536]{0:T(1024)S(1)} %get-tuple-element.388, f32[4,256]{1,0:T(4,128)S(1)} %pad_add_fusion.7, f32[256]{0:T(256)S(1)} %copy-done.77), channel_id=1, replica_groups=mesh['dp'=8,'tensor'=4] {'dp','tensor'}, use_global_device_ids=true, to_apply=%region_26.27 | all-reduce | flops 2816 | bytes 22528 | tf_op jit(solution)/shard_map/psum | solution.py:209
  585.4 20.2 %reduce-scatter.10.cloned.1.call-done = f32[256,1536]{1,0:T(8,128)} async-done(((f32[1024,1536]{1,0:T(8,128)}), f32[256,1536]{1,0:T(8,128)}) %reduce-scatter.10.cloned.1.call-update) | async-done | bytes 1572880 | tf_op jit(solution)/shard_map/reduce_scatter | solution.py:159
  610.0 95.3 %reduce-scatter.20.cloned.1.call-done = f32[768,192]{0,1:T(8,128)} async-done(((f32[768,1536]{0,1:T(8,128)}), f32[768,192]{0,1:T(8,128)}) %reduce-scatter.20.cloned.1.call-update) | async-done | bytes 589840 | tf_op jit(solution)/shard_map/reduce_scatter | solution.py:205
  705.3 99.6 %reduce-scatter.14.cloned.1.call-done = f32[192,768]{1,0:T(8,128)} async-done(((f32[1536,768]{1,0:T(8,128)}), f32[192,768]{1,0:T(8,128)}) %reduce-scatter.14.cloned.1.call-update) | async-done | bytes 589840 | tf_op jit(solution)/shard_map/reduce_scatter | solution.py:201
  804.9 69.0 %reduce-scatter.18.cloned.1.call-done = f32[192,256]{1,0:T(8,128)} async-done(((f32[1536,256]{1,0:T(8,128)}), f32[192,256]{1,0:T(8,128)}) %reduce-scatter.18.cloned.1.call-update) | async-done | bytes 196624 | tf_op jit(solution)/shard_map/reduce_scatter | solution.py:203
  873.9 98.7 %reduce-scatter.16.cloned.1.call-done = f32[192,768]{1,0:T(8,128)} async-done(((f32[1536,768]{1,0:T(8,128)}), f32[192,768]{1,0:T(8,128)}) %reduce-scatter.16.cloned.1.call-update) | async-done | bytes 589840 | tf_op jit(solution)/shard_map/reduce_scatter | solution.py:202
  (383 shorter events, 268.3 us)
Async XLA Ops:
  7.2 74.8 %all-gather.8.cloned.1.call-start = ((), (), s32[]{:S(2)}) async-start(), calls=%async_computation.7 | async-start | bytes 3932160 | tf_op jit(solution)/shard_map/all_gather | solution.py:130
  12.0 69.9 %copy-start.81 = (f32[12]{0:T(128)S(1)}, f32[12]{0:T(128)}, u32[]{:S(2)}) copy-start(f32[12]{0:T(128)} %param.31) | copy-start | bytes 148
  12.1 89.6 %all-gather.10.cloned.1.call-start = ((), (), s32[]{:S(2)}) async-start(), calls=%async_computation.8 | async-start | bytes 2654208 | tf_op jit(solution)/shard_map/all_gather | solution.py:133
  12.8 167.6 %all-gather.12.cloned.1.call-start = ((), (), s32[]{:S(2)}) async-start(), calls=%async_computation.9 | async-start | bytes 2654208 | tf_op jit(solution)/shard_map/all_gather | solution.py:132
  13.6 194.3 %all-gather.14.cloned.1.call-start = ((), (), s32[]{:S(2)}) async-start(), calls=%async_computation.10 | async-start | bytes 2654208 | tf_op jit(solution)/shard_map/all_gather | solution.py:136
  14.1 222.7 %all-gather.16.cloned.1.call-start = ((), (), s32[]{:S(2)}) async-start(), calls=%async_computation.12 | async-start | bytes 3932160 | tf_op jit(solution)/shard_map/all_gather | solution.py:166
  15.2 418.3 %all-gather.18.cloned.1.call-start = ((), (), s32[]{:S(2)}) async-start(), calls=%async_computation.13 | async-start | bytes 5242880 | tf_op jit(solution)/shard_map/all_gather | solution.py:174
  15.9 76.9 %copy-start.60 = (f32[1,256]{1,0:T(1,128)}, f32[1,256]{1,0:T(1,128)S(1)}, u32[]{:S(2)}) copy-start(f32[1,256]{1,0:T(1,128)S(1)} %get-tuple-element.473) | copy-start | bytes 3076
  16.0 76.9 %copy-start.62 = (f32[1,256]{1,0:T(1,128)}, f32[1,256]{1,0:T(1,128)S(1)}, u32[]{:S(2)}) copy-start(f32[1,256]{1,0:T(1,128)S(1)} %get-tuple-element.474) | copy-start | bytes 3076
  16.0 76.9 %copy-start.64 = (f32[1,256]{1,0:T(1,128)}, f32[1,256]{1,0:T(1,128)S(1)}, u32[]{:S(2)}) copy-start(f32[1,256]{1,0:T(1,128)S(1)} %get-tuple-element.475) | copy-start | bytes 3076
  16.0 76.9 %copy-start.66 = (f32[1,256]{1,0:T(1,128)}, f32[1,256]{1,0:T(1,128)S(1)}, u32[]{:S(2)}) copy-start(f32[1,256]{1,0:T(1,128)S(1)} %get-tuple-element.476) | copy-start | bytes 3076
  16.0 90.9 %copy-start.46 = (f32[768]{0:T(1024)}, f32[768]{0:T(1024)S(1)}, u32[]{:S(2)}) copy-start(f32[768]{0:T(1024)S(1)} %get-tuple-element.397) | copy-start | bytes 9220
  16.0 90.9 %copy-start.48 = (f32[768]{0:T(1024)}, f32[768]{0:T(1024)S(1)}, u32[]{:S(2)}) copy-start(f32[768]{0:T(1024)S(1)} %get-tuple-element.398) | copy-start | bytes 9220
  16.1 90.9 %copy-start.50 = (f32[768]{0:T(1024)}, f32[768]{0:T(1024)S(1)}, u32[]{:S(2)}) copy-start(f32[768]{0:T(1024)S(1)} %get-tuple-element.399) | copy-start | bytes 9220
  16.1 90.8 %copy-start.52 = (f32[768]{0:T(1024)}, f32[768]{0:T(1024)S(1)}, u32[]{:S(2)}) copy-start(f32[768]{0:T(1024)S(1)} %get-tuple-element.400) | copy-start | bytes 9220
  146.5 166.9 %copy-start.41 = (f32[4,256,12]{1,2,0:T(8,128)}, f32[4,256,12]{1,2,0:T(8,128)S(1)}, u32[]{:S(2)}) copy-start(f32[4,256,12]{1,2,0:T(8,128)S(1)} %copy.382) | copy-start | bytes 147460
  349.3 188.0 %reduce-scatter.22.cloned.1.call-start = ((), (), s32[]{:S(2)}) async-start(), calls=%async_computation.19 | async-start | bytes 884736
  418.5 124.9 %reduce-scatter.12.cloned.1.call-start = ((), (), s32[]{:S(2)}) async-start(), calls=%async_computation.14 | async-start | bytes 7864320 | tf_op jit(solution)/shard_map/reduce_scatter | solution.py:186
  446.5 159.0 %reduce-scatter.10.cloned.1.call-start = ((), (), s32[]{:S(2)}) async-start(), calls=%async_computation.11 | async-start | bytes 7864320 | tf_op jit(solution)/shard_map/reduce_scatter | solution.py:159
  455.1 250.2 %reduce-scatter.20.cloned.1.call-start = ((), (), s32[]{:S(2)}) async-start(), calls=%async_computation.18 | async-start | bytes 5308416 | tf_op jit(solution)/shard_map/reduce_scatter | solution.py:205
  463.0 341.9 %reduce-scatter.14.cloned.1.call-start = ((), (), s32[]{:S(2)}) async-start(), calls=%async_computation.15 | async-start | bytes 5308416 | tf_op jit(solution)/shard_map/reduce_scatter | solution.py:201
  470.5 403.5 %reduce-scatter.18.cloned.1.call-start = ((), (), s32[]{:S(2)}) async-start(), calls=%async_computation.17 | async-start | bytes 1769472 | tf_op jit(solution)/shard_map/reduce_scatter | solution.py:203
  474.6 498.0 %reduce-scatter.16.cloned.1.call-start = ((), (), s32[]{:S(2)}) async-start(), calls=%async_computation.16 | async-start | bytes 5308416 | tf_op jit(solution)/shard_map/reduce_scatter | solution.py:202
  497.4 108.2 %copy-start.74 = (f32[256]{0:T(256)S(1)}, f32[256]{0:T(256)}, u32[]{:S(2)}) copy-start(f32[256]{0:T(256)} %get-tuple-element.477) | copy-start | bytes 3076
  (79 other events, 992.6 us)
Sparse Core Ops, SparseCore 0:
  12.2 31.2 all-gather.7
  45.6 55.9 all-gather.9
  103.8 51.5 all-gather.11
  157.4 50.3 all-gather.13
  209.8 27.0 all-gather.15
  349.4 35.5 all-gather.17
  418.6 64.2 reduce-scatter.21
  485.5 57.9 reduce-scatter.11
  546.0 59.5 reduce-scatter.9
  609.6 95.6 reduce-scatter.19
  709.5 95.3 reduce-scatter.13
  808.8 65.1 reduce-scatter.17
  878.2 94.4 reduce-scatter.15
